TPU v7x, 32 devices: a whole 2x2x4 slice. The times are simulated.
32 devices in a mesh: seq: 8 (over z, y), tp: 4 (over x, core).
Axes of the slice: x: 2, y: 2, z: 4, core: 2. Of those that a mesh axis runs over, the one named last changes fastest.
Arguments:
- prefill_tokens: bfloat16 [4096, 2304], P('seq'), may hold values from -6 to 6
- decode_tokens: bfloat16 [64, 2304], P('seq'), may hold values from -6 to 6
- attention_gain: float32 [2304], replicated, may hold values from 0.5 to 1.5
- qkv_weight: bfloat16 [2304, 3, 2304], P(None, None, 'tp'), may hold values from -0.125 to 0.125
- out_weight: bfloat16 [2304, 2304], P('tp'), may hold values from -0.375 to 0.375
- feedforward_gain: float32 [2304], replicated, may hold values from 0.5 to 1.5
- prefill_cache: bfloat16 [8, 2, 1024, 2304], P('seq', None, None, 'tp'), may hold values from -420 to 420
- prefill_offsets: int32 [8], P('seq'), may hold values from 0 to 1024, as said below
- decode_cache: bfloat16 [64, 2, 256, 2304], P('seq', None, None, 'tp'), may hold values from -420 to 420
- decode_lengths: int32 [64], P('seq'), may hold values from 1 to 256, as said below
- request_slot: int32 [64], replicated, may hold values from 0 to 63, each once
Outputs:
- prefill_hidden: bfloat16 [4096, 2304], P('seq')
- decode_hidden: bfloat16 [64, 2304], P('seq')
- prefill_normed: bfloat16 [4096, 2304], P('seq')
- decode_normed: bfloat16 [64, 2304], P('seq')
Inputs may be any that keep to these rules, and one draw needn't show every extreme that they name: `request_slot`: each slot is named by exactly one request. `decode_lengths`: some slot holds exactly 256 positions. `prefill_offsets`: some request has exactly 1024 cached positions.
All inputs are finite; a program needn't handle non-finite values.
Results may differ from a plain program's by a relative error of at most 0.014.
The roundings to bfloat16 on the way count: a program that leaves them out, or rounds other values in their place, can miss the bound.
Values may be sent and summed in bfloat16 or wider, within the bound.
A program may use at most 128 MiB of HBM per device.

v0:
```python
import math
import jax
import jax.numpy as jnp
from jax import lax
from jax.sharding import PartitionSpec as P

HEAD = 64
RMS_EPSILON = 1e-05
ROPE_BASE = 10000.0
NEGATIVE = -1e30


def rms_norm(stream, gain):
    widened = stream.astype(jnp.float32)
    inverse = lax.rsqrt(jnp.mean(widened * widened, axis=-1, keepdims=True) + RMS_EPSILON)
    return widened * inverse * gain


def rotate(vectors, positions):
    half_dim = vectors.shape[-1] // 2
    exponent = jnp.arange(half_dim, dtype=jnp.float32) * (2.0 / vectors.shape[-1])
    frequency = ROPE_BASE ** (-exponent)
    angles = positions[:, None] * frequency[None, :]
    cosine = jnp.cos(angles)[:, None, :]
    sine_part = jnp.sin(angles)[:, None, :]
    first_half = vectors[..., :half_dim]
    second_half = vectors[..., half_dim:]
    return jnp.concatenate(
        [
            first_half * cosine - second_half * sine_part,
            second_half * cosine + first_half * sine_part,
        ],
        axis=-1,
    )


def prefill_attention(block_rows, cache_pair, offset, head_count):
    span_rows = block_rows.shape[0]
    cache_len = cache_pair.shape[1]
    score_scale = 1.0 / math.sqrt(HEAD)
    positions = offset.astype(jnp.float32) + jnp.arange(span_rows, dtype=jnp.float32)
    queries = rotate(
        block_rows[:, 0].reshape(span_rows, head_count, HEAD).astype(jnp.float32), positions
    ).astype(jnp.bfloat16)
    new_keys = rotate(
        block_rows[:, 1].reshape(span_rows, head_count, HEAD).astype(jnp.float32), positions
    ).astype(jnp.bfloat16)
    new_values = block_rows[:, 2].reshape(span_rows, head_count, HEAD)
    cache_keys = cache_pair[0].reshape(cache_len, head_count, HEAD)
    cache_values = cache_pair[1].reshape(cache_len, head_count, HEAD)
    cache_scores = (
        jnp.einsum("qhe,khe->hqk", queries, cache_keys, preferred_element_type=jnp.float32)
        * score_scale
    )
    span_scores = (
        jnp.einsum("qhe,khe->hqk", queries, new_keys, preferred_element_type=jnp.float32)
        * score_scale
    )
    cache_visible = (jnp.arange(cache_len, dtype=jnp.int32) < offset)[None, None, :]
    causal = (
        jnp.arange(span_rows, dtype=jnp.int32)[None, :]
        <= jnp.arange(span_rows, dtype=jnp.int32)[:, None]
    )[None]
    cache_scores = jnp.where(cache_visible, cache_scores, NEGATIVE)
    span_scores = jnp.where(causal, span_scores, NEGATIVE)
    row_peak = jnp.maximum(
        jnp.max(cache_scores, axis=-1, keepdims=True), jnp.max(span_scores, axis=-1, keepdims=True)
    )
    cache_exp = jnp.exp(cache_scores - row_peak)
    span_exp = jnp.exp(span_scores - row_peak)
    denominator = jnp.sum(cache_exp, axis=-1, keepdims=True) + jnp.sum(
        span_exp, axis=-1, keepdims=True
    )
    cache_weights = (cache_exp / denominator).astype(jnp.bfloat16)
    span_weights = (span_exp / denominator).astype(jnp.bfloat16)
    attended = jnp.einsum(
        "hqk,khe->qhe", cache_weights, cache_values, preferred_element_type=jnp.float32
    )
    attended = attended + jnp.einsum(
        "hqk,khe->qhe", span_weights, new_values, preferred_element_type=jnp.float32
    )
    return attended.reshape(span_rows, head_count * HEAD).astype(jnp.bfloat16)


def decode_attention(routed, cache_block, lengths, head_count):
    slot_count = routed.shape[0]
    cache_len = cache_block.shape[2]
    score_scale = 1.0 / math.sqrt(HEAD)
    positions = lengths.astype(jnp.float32)
    queries = rotate(
        routed[:, 0].reshape(slot_count, head_count, HEAD).astype(jnp.float32), positions
    ).astype(jnp.bfloat16)
    new_keys = rotate(
        routed[:, 1].reshape(slot_count, head_count, HEAD).astype(jnp.float32), positions
    ).astype(jnp.bfloat16)
    new_values = routed[:, 2].reshape(slot_count, head_count, HEAD)
    cache_keys = cache_block[:, 0].reshape(slot_count, cache_len, head_count, HEAD)
    cache_values = cache_block[:, 1].reshape(slot_count, cache_len, head_count, HEAD)
    cache_scores = (
        jnp.einsum("she,skhe->shk", queries, cache_keys, preferred_element_type=jnp.float32)
        * score_scale
    )
    self_scores = (
        jnp.einsum("she,she->sh", queries, new_keys, preferred_element_type=jnp.float32)
        * score_scale
    )
    visible = (jnp.arange(cache_len, dtype=jnp.int32)[None, :] < lengths[:, None])[:, None, :]
    cache_scores = jnp.where(visible, cache_scores, NEGATIVE)
    row_peak = jnp.maximum(jnp.max(cache_scores, axis=-1), self_scores)
    cache_exp = jnp.exp(cache_scores - row_peak[..., None])
    self_exp = jnp.exp(self_scores - row_peak)
    denominator = jnp.sum(cache_exp, axis=-1) + self_exp
    cache_weights = (cache_exp / denominator[..., None]).astype(jnp.bfloat16)
    self_weights = (self_exp / denominator).astype(jnp.bfloat16)
    attended = jnp.einsum(
        "shk,skhe->she", cache_weights, cache_values, preferred_element_type=jnp.float32
    )
    attended = attended + self_weights.astype(jnp.float32)[..., None] * new_values.astype(
        jnp.float32
    )
    return attended.reshape(slot_count, head_count * HEAD).astype(jnp.bfloat16)


def local(
    prefill_tokens,
    decode_tokens,
    attention_gain,
    qkv_weight,
    out_weight,
    feedforward_gain,
    prefill_cache,
    prefill_offsets,
    decode_cache,
    decode_lengths,
    request_slot,
):
    span_rows = prefill_tokens.shape[0]
    decode_rows = decode_tokens.shape[0]
    model_width = prefill_tokens.shape[1]
    local_width = out_weight.shape[0]
    head_count = local_width // HEAD
    tokens_all = jnp.concatenate([prefill_tokens, decode_tokens], axis=0)
    normed_in = rms_norm(tokens_all, attention_gain).astype(jnp.bfloat16)
    projected = jnp.dot(
        normed_in,
        qkv_weight.reshape(model_width, 3 * local_width),
        preferred_element_type=jnp.float32,
    ).astype(jnp.bfloat16)
    projected = projected.reshape(-1, 3, local_width)
    prefill_block = projected[:span_rows]
    decode_block = projected[span_rows:]
    seq_rank = lax.axis_index("seq")
    own_slots = seq_rank * decode_rows + jnp.arange(decode_rows, dtype=jnp.int32)
    arrived = lax.all_gather(decode_block, "seq", axis=0, tiled=True)
    picker = (request_slot[None, :] == own_slots[:, None]).astype(jnp.bfloat16)
    routed = jnp.einsum("sr,rcw->scw", picker, arrived, preferred_element_type=jnp.float32).astype(
        jnp.bfloat16
    )
    slot_results = decode_attention(routed, decode_cache, decode_lengths, head_count)
    prefill_attended = prefill_attention(
        prefill_block, prefill_cache[0], prefill_offsets[0], head_count
    )
    my_slots = lax.dynamic_slice_in_dim(request_slot, seq_rank * decode_rows, decode_rows)
    shard_piece = lax.all_gather(slot_results, "seq", axis=0, tiled=True)
    slot_ids = jnp.arange(shard_piece.shape[0], dtype=jnp.int32)
    picker = (my_slots[:, None] == slot_ids[None, :]).astype(jnp.bfloat16)
    returned = jnp.dot(picker, shard_piece, preferred_element_type=jnp.float32).astype(jnp.bfloat16)
    attended_all = jnp.concatenate([prefill_attended, returned], axis=0)
    partial_value = jnp.dot(attended_all, out_weight, preferred_element_type=jnp.float32)
    combined = lax.psum(partial_value.astype(jnp.bfloat16), "tp").astype(jnp.float32)
    hidden = (tokens_all.astype(jnp.float32) + combined).astype(jnp.bfloat16)
    normed = rms_norm(hidden, feedforward_gain).astype(jnp.bfloat16)
    return (hidden[:span_rows], hidden[span_rows:], normed[:span_rows], normed[span_rows:])


def solution(mesh):
    placed = (
        P("seq", None),
        P("seq", None),
        P(),
        P(None, None, "tp"),
        P("tp", None),
        P(),
        P("seq", None, None, "tp"),
        P("seq"),
        P("seq", None, None, "tp"),
        P("seq"),
        P(),
    )
    return jax.shard_map(
        local,
        mesh=mesh,
        in_specs=placed,
        out_specs=(P("seq", None), P("seq", None), P("seq", None), P("seq", None)),
        check_vma=False,
    )
```

profile of v0, /device:TPU:0, one launch (start us, length us, event | category | flops | bytes accessed | tf_op | source)
XLA Modules:
  0.0 215.5 jit_solution(18062923695454391334)
XLA Ops:
  7.2 0.8 convert_element_type.115
  8.1 0.7 iota_compare_fusion.1
  8.8 2.4 %fusion.8 = f32[520]{0:T(1024)S(1)} fusion(bf16[8,2304]{1,0:T(8,128)(2,1)} %param.12, bf16[512,2304]{1,0:T(8,128)(2,1)} %param.11), kind=kLoop, calls=%fused_computation.19 | loop fusion | flops 7187960 | bytes 2398240 | tf_op jit(solution)/shard_map/reduce_sum | solution.py:15
  11.2 8.6 %convolution_convert_fusion.1 = bf16[520,1728]{1,0:T(8,128)(2,1)S(1)} fusion(bf16[2304,1728]{0,1:T(8,128)(2,1)} %bitcast.71, f32[2304]{0:T(1024)} %param.13, f32[520]{0:T(1024)S(1)} %add_rsqrt_fusion.1, bf16[8,2304]{1,0:T(8,128)(2,1)} %param.12, bf16[512,2304]{1,0:T(8,128)(2,1)} %param.11), kind=kOutput, calls=%fused_computation.25 | convolution fusion | flops 4149849600 | bytes 12167200 | tf_op jit(solution)/shard_map/dot_general | solution.py:144
  19.8 1.4 slice.106
  21.2 0.1 iota_compare_fusion
  21.3 2.5 %fusion.55 = (bf16[8,1,256,576]{2,3,1,0:T(8,128)(2,1)}, bf16[8,1,256,576]{2,3,1,0:T(8,128)(2,1)}) fusion(bf16[8,2,256,576]{2,3,1,0:T(8,128)(2,1)S(1)} %bitcast.64), kind=kLoop, calls=%fused_computation.103 | loop fusion | bytes 9437184 | tf_op jit(solution)/shard_map/slice | solution.py:97
  23.8 0.1 slice.92
  23.9 32.5 %all_gather.6 = bf16[64,3,576]{2,0,1:T(8,128)(2,1)S(1)} all-gather(bf16[8,3,576]{2,0,1:T(8,128)(2,1)S(1)} %copy.25), channel_id=1, replica_groups=mesh['seq'=8,'tp'=4] {'seq'}, dimensions={0}, use_global_device_ids=true | all-gather | bytes 248832 | tf_op jit(solution)/shard_map/all_gather | solution.py:154
  56.5 0.2 convolution_convert_fusion.2
  56.7 0.1 reshape.210
  56.8 0.1 multiply_cosine_fusion.1
  56.9 0.1 subtract_convert_fusion.2
  57.1 0.1 fusion.38
  57.2 0.2 fusion.32
  57.3 0.1 copy.34
  57.4 2.1 fusion.35
  59.5 0.1 fusion.34
  59.6 0.2 fusion.33
  59.8 0.1 fusion.37
  59.9 0.1 reshape.211
  60.1 2.4 %fusion.29 = f32[8,9,1,64]{3,2,1,0:T(1,128)S(1)} fusion(bf16[8,256,9,64]{1,3,2,0:T(8,128)(2,1)} %bitcast.68, bf16[8,9,256,1]{2,0,1,3:T(8,128)(2,1)S(1)} %fusion.37), kind=kOutput, calls=%fused_computation.53 | convolution fusion | flops 2359296 | bytes 2414592 | tf_op jit(solution)/shard_map/shk,skhe->she/dot_general | solution.py:115
  62.4 0.1 fusion.31
  62.5 0.1 convert_element_type.124
  62.6 30.5 %all_gather.7 = bf16[64,576]{1,0:T(8,128)(2,1)S(1)} all-gather(bf16[8,576]{1,0:T(8,128)(2,1)S(1)} %convert_element_type.124), channel_id=1, replica_groups=mesh['seq'=8,'tp'=4] {'seq'}, dimensions={0}, use_global_device_ids=true | all-gather | bytes 82944 | tf_op jit(solution)/shard_map/all_gather | solution.py:164
  93.2 0.2 convolution_convert_fusion.3
  93.4 0.8 copy.27
  94.2 3.2 %fusion.56 = (bf16[1,1,1024,576]{2,3,1,0:T(8,128)(2,1)}, bf16[1,1,1024,576]{2,3,1,0:T(8,128)(2,1)}) fusion(bf16[1,2,1024,576]{2,3,1,0:T(8,128)(2,1)} %param.17), kind=kLoop, calls=%fused_computation.104 | loop fusion | bytes 4718592 | tf_op jit(solution)/shard_map/slice | solution.py:49
  98.1 4.0 %copy.23 = bf16[512,1728]{0,1:T(8,128)(2,1)} copy(bf16[512,1728]{1,0:T(8,128)(2,1)} %slice.106) | data formatting | bytes 3538944 | tf_op jit(solution)/shard_map/slice | solution.py:150
  102.1 2.4 %fusion.57 = (bf16[512,1,576]{0,2,1:T(8,128)(2,1)}, bf16[512,1,576]{0,2,1:T(8,128)(2,1)S(1)}, bf16[512,1,576]{0,2,1:T(8,128)(2,1)S(1)}) fusion(bf16[512,3,576]{0,2,1:T(8,128)(2,1)} %bitcast.62), kind=kLoop, calls=%fused_computation.105 | loop fusion | bytes 3538944 | tf_op jit(solution)/shard_map/slice | solution.py:48
  104.5 1.2 convert.40
  105.6 0.3 multiply_cosine_fusion
  105.9 0.1 convert.39
  106.1 1.6 subtract_convert_fusion
  107.7 2.8 %fusion = (f32[9,512]{1,0:T(8,128)S(1)}, f32[9,512,1024]{2,1,0:T(8,128)S(1)}) fusion(pred[1024]{0:T(1024)(128)(4,1)S(1)} %iota_compare_fusion.3, bf16[1024,9,64]{0,2,1:T(8,128)(2,1)S(1)} %bitcast.65, bf16[512,9,32]{0,2,1:T(8,128)(2,1)S(1)} %get-tuple-element.17, bf16[512,9,32]{0,2,1:T(8,128)(2,1)S(1)} %get-tuple-element.18), kind=kOutput, calls=%fused_computation.3 | convolution fusion | flops 619310592 | bytes 20663296 | tf_op jit(solution)/shard_map/qhe,khe->hqk/dot_general | solution.py:52
  110.5 5.3 %fusion.3 = (f32[9,512]{1,0:T(8,128)S(1)}, f32[9,512,512]{1,2,0:T(8,128)}) fusion(pred[512,512]{0,1:T(8,128)(4,1)S(1)} %iota_compare_fusion, bf16[512,9,32]{0,2,1:T(8,128)(2,1)S(1)} %get-tuple-element.14, bf16[512,9,32]{0,2,1:T(8,128)(2,1)S(1)} %get-tuple-element.13, bf16[512,9,32]{0,2,1:T(8,128)(2,1)S(1)} %get-tuple-element.17, ...), kind=kOutput, calls=%fused_computation.9 | convolution fusion | flops 311422464 | bytes 10897408 | tf_op jit(solution)/shard_map/qhe,khe->hqk/dot_general | solution.py:56
  115.8 4.5 %fusion.1 = f32[9,512]{1,0:T(8,128)S(1)} fusion(f32[9,512,1024]{2,1,0:T(8,128)S(1)} %get-tuple-element.35, f32[9,512]{1,0:T(8,128)S(1)} %max.11, pred[1024]{0:T(1024)(128)(4,1)S(1)} %iota_compare_fusion.3), kind=kLoop, calls=%fused_computation.4 | loop fusion | flops 18869760 | bytes 18912256 | tf_op jit(solution)/shard_map/reduce_sum | solution.py:71
  120.4 5.6 %fusion.4 = f32[9,512]{1,0:T(8,128)S(1)} fusion(f32[9,512,512]{1,2,0:T(8,128)} %get-tuple-element.37, f32[9,512]{1,0:T(8,128)S(1)} %max.11, pred[512,512]{0,1:T(8,128)(4,1)S(1)} %iota_compare_fusion), kind=kLoop, calls=%fused_computation.10 | loop fusion | flops 9432576 | bytes 9736192 | tf_op jit(solution)/shard_map/reduce_sum | solution.py:71
  126.0 7.1 %fusion.16 = f32[512,9,64]{0,2,1:T(8,128)} fusion(bf16[1024,9,64]{0,2,1:T(8,128)(2,1)} %bitcast.69, f32[9,512,1024]{2,1,0:T(8,128)S(1)} %get-tuple-element.35, f32[9,512]{1,0:T(8,128)S(1)} %add.78, f32[9,512]{1,0:T(8,128)S(1)} %max.11, pred[1024]{0:T(1024)(128)(4,1)S(1)} %iota_compare_fusion.3), kind=kOutput, calls=%fused_computation.29 | convolution fusion | flops 627572736 | bytes 21271552 | tf_op jit(solution)/shard_map/hqk,khe->qhe/dot_general | solution.py:76
  133.1 6.0 %fusion.19 = bf16[512,9,64]{0,2,1:T(8,128)(2,1)S(1)} fusion(f32[512,9,64]{0,2,1:T(8,128)} %fusion.16, bf16[512,9,64]{0,2,1:T(8,128)(2,1)S(1)} %bitcast.70, f32[9,512,512]{1,2,0:T(8,128)} %get-tuple-element.37, f32[9,512]{1,0:T(8,128)S(1)} %add.78, f32[9,512]{1,0:T(8,128)S(1)} %max.11, pred[512,512]{0,1:T(8,128)(4,1)S(1)} %iota_compare_fusion), kind=kOutput, calls=%fused_computation.32 | convolution fusion | flops 314376192 | bytes 12095488 | tf_op jit(solution)/shard_map/hqk,khe->qhe/dot_general | solution.py:79
  139.1 3.5 %convolution_convert_fusion = bf16[520,2304]{1,0:T(8,128)(2,1)} fusion(bf16[576,2304]{1,0:T(8,128)(2,1)S(1)} %copy-done, bf16[8,576]{0,1:T(8,128)(2,1)S(1)} %copy-done.4, bf16[512,576]{0,1:T(8,128)(2,1)S(1)} %bitcast.72), kind=kOutput, calls=%fused_computation.24 | convolution fusion | flops 1382584320 | bytes 5649408 | tf_op jit(solution)/shard_map/dot_general | solution.py:169
  142.6 57.6 %all-reduce.2.cloned.1.call-done = bf16[520,2304]{1,0:T(8,128)(2,1)} async-done(((bf16[520,2304]{1,0:T(8,128)(2,1)}), bf16[520,2304]{1,0:T(8,128)(2,1)}) %all-reduce.2.cloned.1.call-update) | async-done | bytes 2396176 | tf_op jit(solution)/shard_map/psum | solution.py:170
  200.2 3.4 %fusion.5 = (f32[520]{0:T(1024)S(1)}, bf16[520,2304]{1,0:T(8,128)(2,1)S(1)}) fusion(bf16[520,2304]{1,0:T(8,128)(2,1)} %all-reduce.2.cloned.1.call-done, bf16[8,2304]{1,0:T(8,128)(2,1)S(1)} %copy-done.3, bf16[512,2304]{1,0:T(8,128)(2,1)} %param.11), kind=kLoop, calls=%fused_computation.16 | loop fusion | flops 11980280 | bytes 7190560 | tf_op jit(solution)/shard_map/reduce_sum | solution.py:15
  203.6 1.6 slice.122
  205.2 0.6 slice.123
  205.8 0.6 fusion.7
  206.4 1.6 slice.124
  208.0 0.6 slice.125
  (37 shorter events, 0.4 us)
Async XLA Ops:
  7.2 131.9 %copy-start = (bf16[576,2304]{1,0:T(8,128)(2,1)S(1)}, bf16[576,2304]{1,0:T(8,128)(2,1)}, u32[]{:S(2)}) copy-start(bf16[576,2304]{1,0:T(8,128)(2,1)} %param.15) | copy-start | bytes 7962628
  7.2 193.0 %all-reduce.2.cloned.1.call-start = ((), (), s32[]{:S(2)}) async-start(), calls=%async_computation | async-start | bytes 4792320 | tf_op jit(solution)/shard_map/psum | solution.py:170
  8.8 12.5 %slice-start = ((s8[4718592]{0:T(1024)(128)(4,1)}), s8[4194304]{0:T(1024)(128)(4,1)S(1)}, s32[]{:S(2)}) async-start(s8[4718592]{0:T(1024)(128)(4,1)} %bitcast.63), calls=%async_computation.1 | async-start | bytes 8388608
  11.2 10.1 %slice-start.1 = ((s8[4718592]{0:T(1024)(128)(4,1)}), s8[524288]{0:T(1024)(128)(4,1)S(1)}, s32[]{:S(2)}) async-start(s8[4718592]{0:T(1024)(128)(4,1)} %bitcast.63), calls=%async_computation.2 | async-start | bytes 1048576
  21.3 35.1 %copy-start.6 = (s32[64]{0:T(128)S(1)}, s32[64]{0:T(128)}, u32[]{:S(2)}) copy-start(s32[64]{0:T(128)} %param.21) | copy-start | bytes 772
  105.6 2.1 copy-start.1
  126.0 7.1 %copy-start.2 = (bf16[512,1,576]{0,2,1:T(8,128)(2,1)S(1)}, bf16[512,1,576]{0,2,1:T(8,128)(2,1)}, u32[]{:S(2)}) copy-start(bf16[512,1,576]{0,2,1:T(8,128)(2,1)} %get-tuple-element.10) | copy-start | bytes 1769476
  133.1 6.0 %copy-start.4 = (bf16[8,576]{0,1:T(8,128)(2,1)S(1)}, bf16[8,576]{0,1:T(8,128)(2,1)}, u32[]{:S(2)}) copy-start(bf16[8,576]{0,1:T(8,128)(2,1)} %copy.27) | copy-start | bytes 27652
  139.1 61.1 %copy-start.3 = (bf16[8,2304]{1,0:T(8,128)(2,1)S(1)}, bf16[8,2304]{1,0:T(8,128)(2,1)}, u32[]{:S(2)}) copy-start(bf16[8,2304]{1,0:T(8,128)(2,1)} %param.12) | copy-start | bytes 110596
  142.6 63.2 %copy-start.5 = (f32[2304]{0:T(1024)S(1)}, f32[2304]{0:T(1024)}, u32[]{:S(2)}) copy-start(f32[2304]{0:T(1024)} %param.16) | copy-start | bytes 27652
Sparse Core Ops, SparseCore 0:
  142.8 57.4 all-reduce.1
where the time goes:
time: 216 us; the launch traced here: 215 us
  blocking collectives  63.1 us (29%)
  waiting for transfers between devices  57.6 us (27%)
  matrix products  38.1 us (18%)
  other arithmetic  22.4 us (10%)
  local copies, waits for them, and re-layouts  19.3 us (9%)
  between operations  15 us (7%)
    psum x1, waiting for transfers between devices, local(): lax.psum(partial_value.astype(jnp.bfloat16), 'tp').astype(jnp.float32)  57.6 us
    all_gather x1, blocking collectives, local(): arrived = lax.all_gather(decode_block, 'seq', axis=0, tiled=True)  32.5 us
    all_gather x1, blocking collectives, local(): shard_piece = lax.all_gather(slot_results, 'seq', axis=0, tiled=True)  30.5 us
    dot_general x1, matrix products, local(): jnp.dot(normed_in, qkv_weight.reshape(model_width, 3 * local_width), pref...  8.62 us
    dot_general x1, matrix products, prefill_attention(): jnp.einsum('hqk,khe->qhe', cache_weights, cache_values, preferred_element...  7.07 us
    dot_general x1, matrix products, prefill_attention(): jnp.einsum('hqk,khe->qhe', span_weights, new_values, preferred_element_ty...  6 us
    reduce_sum x2, other arithmetic, rms_norm(): jnp.mean(widened * widened, axis=-1, keepdims=True) + RMS_EPSILON  5.77 us
    reduce_sum x1, other arithmetic, prefill_attention(): jnp.sum(span_exp, axis=-1, keepdims=True)  5.61 us
  transfers between devices with their start and end apart: 1, of which 1 were waited for; matrix products, arithmetic and copies ran while one was open for 0% of the time, Pallas kernels for 0%

commit v1 on v0

--- a/solution.py
+++ b/solution.py
@@ -167,7 +167,9 @@
     returned = jnp.dot(picker, shard_piece, preferred_element_type=jnp.float32).astype(jnp.bfloat16)
     attended_all = jnp.concatenate([prefill_attended, returned], axis=0)
     partial_value = jnp.dot(attended_all, out_weight, preferred_element_type=jnp.float32)
-    combined = lax.psum(partial_value.astype(jnp.bfloat16), "tp").astype(jnp.float32)
+    combined = jnp.sum(lax.all_gather(partial_value.astype(jnp.bfloat16), "tp"), axis=0).astype(
+        jnp.float32
+    )
     hidden = (tokens_all.astype(jnp.float32) + combined).astype(jnp.bfloat16)
     normed = rms_norm(hidden, feedforward_gain).astype(jnp.bfloat16)
     return (hidden[:span_rows], hidden[span_rows:], normed[:span_rows], normed[span_rows:])

time: 216 us -> 232 us (1.074)
  waiting for transfers between devices: 57.6 us -> 66.1 us
  other arithmetic: 22.4 us -> 29.7 us
    all_gather x0 -> x1, waiting for transfers between devices: none -> 66.1 us  [local(): lax.all_gather(partial_value.astype(jnp.bfloat16), 'tp')]
    psum x1 -> x0, waiting for transfers between devices: 57.6 us -> none  [local(): lax.psum(partial_value.astype(jnp.bfloat16), 'tp').astype(jnp.float32)]
    reduce_sum x0 -> x1, other arithmetic: none -> 7.33 us  [local(): jnp.sum(lax.all_gather(partial_value.astype(jnp.bfloat16), 'tp'), axis=0)]
where the time goes in v1:
time: 232 us; the launch traced here: 231 us
  waiting for transfers between devices  66.1 us (28%)
  blocking collectives  63.1 us (27%)
  matrix products  38.1 us (16%)
  other arithmetic  29.7 us (13%)
  local copies, waits for them, and re-layouts  19.3 us (8%)
  between operations  14.9 us (6%)
    all_gather x1, waiting for transfers between devices, local(): lax.all_gather(partial_value.astype(jnp.bfloat16), 'tp')  66.1 us
    all_gather x1, blocking collectives, local(): arrived = lax.all_gather(decode_block, 'seq', axis=0, tiled=True)  32.5 us
    all_gather x1, blocking collectives, local(): shard_piece = lax.all_gather(slot_results, 'seq', axis=0, tiled=True)  30.5 us
    dot_general x1, matrix products, local(): jnp.dot(normed_in, qkv_weight.reshape(model_width, 3 * local_width), pref...  8.62 us
    reduce_sum x1, other arithmetic, local(): jnp.sum(lax.all_gather(partial_value.astype(jnp.bfloat16), 'tp'), axis=0)  7.33 us
    dot_general x1, matrix products, prefill_attention(): jnp.einsum('hqk,khe->qhe', cache_weights, cache_values, preferred_element...  7.07 us
    dot_general x1, matrix products, prefill_attention(): jnp.einsum('hqk,khe->qhe', span_weights, new_values, preferred_element_ty...  6 us
    reduce_sum x2, other arithmetic, rms_norm(): jnp.mean(widened * widened, axis=-1, keepdims=True) + RMS_EPSILON  5.79 us
  transfers between devices with their start and end apart: 1, of which 1 were waited for; matrix products, arithmetic and copies ran while one was open for 0% of the time, Pallas kernels for 0%

profile of v1, /device:TPU:0, one launch (start us, length us, event | category | flops | bytes accessed | tf_op | source)
XLA Modules:
  0.0 231.3 jit_solution(11094251642154847372)
XLA Ops:
  7.2 0.8 convert_element_type.117
  8.1 0.7 iota_compare_fusion.1
  8.8 2.4 %fusion.8 = f32[520]{0:T(1024)S(1)} fusion(bf16[8,2304]{1,0:T(8,128)(2,1)} %param.12, bf16[512,2304]{1,0:T(8,128)(2,1)} %param.11), kind=kLoop, calls=%fused_computation.19 | loop fusion | flops 7187960 | bytes 2398240 | tf_op jit(solution)/shard_map/reduce_sum | solution.py:15
  11.2 8.6 %convolution_convert_fusion.1 = bf16[520,1728]{1,0:T(8,128)(2,1)S(1)} fusion(bf16[2304,1728]{0,1:T(8,128)(2,1)} %bitcast.73, f32[2304]{0:T(1024)} %param.13, f32[520]{0:T(1024)S(1)} %add_rsqrt_fusion.1, bf16[8,2304]{1,0:T(8,128)(2,1)} %param.12, bf16[512,2304]{1,0:T(8,128)(2,1)} %param.11), kind=kOutput, calls=%fused_computation.25 | convolution fusion | flops 4149849600 | bytes 12167200 | tf_op jit(solution)/shard_map/dot_general | solution.py:144
  19.8 1.4 slice.106
  21.2 0.1 iota_compare_fusion
  21.3 2.5 %fusion.55 = (bf16[8,1,256,576]{2,3,1,0:T(8,128)(2,1)}, bf16[8,1,256,576]{2,3,1,0:T(8,128)(2,1)}) fusion(bf16[8,2,256,576]{2,3,1,0:T(8,128)(2,1)S(1)} %bitcast.66), kind=kLoop, calls=%fused_computation.103 | loop fusion | bytes 9437184 | tf_op jit(solution)/shard_map/slice | solution.py:97
  23.8 0.1 slice.92
  23.9 32.5 %all_gather.12 = bf16[64,3,576]{2,0,1:T(8,128)(2,1)S(1)} all-gather(bf16[8,3,576]{2,0,1:T(8,128)(2,1)S(1)} %copy.25), channel_id=1, replica_groups=mesh['seq'=8,'tp'=4] {'seq'}, dimensions={0}, use_global_device_ids=true | all-gather | bytes 248832 | tf_op jit(solution)/shard_map/all_gather | solution.py:154
  56.5 0.2 convolution_convert_fusion.2
  56.7 0.1 reshape.210
  56.8 0.1 multiply_cosine_fusion.1
  57.0 0.1 subtract_convert_fusion.2
  57.1 0.1 fusion.38
  57.2 0.2 fusion.32
  57.3 0.1 copy.34
  57.4 2.1 fusion.35
  59.5 0.1 fusion.34
  59.6 0.2 fusion.33
  59.8 0.1 fusion.37
  60.1 2.4 %fusion.29 = f32[8,9,1,64]{3,2,1,0:T(1,128)S(1)} fusion(bf16[8,256,9,64]{1,3,2,0:T(8,128)(2,1)} %bitcast.70, bf16[8,9,256,1]{2,0,1,3:T(8,128)(2,1)S(1)} %fusion.37), kind=kOutput, calls=%fused_computation.53 | convolution fusion | flops 2359296 | bytes 2414592 | tf_op jit(solution)/shard_map/shk,skhe->she/dot_general | solution.py:115
  62.4 0.1 fusion.31
  62.5 0.1 convert_element_type.126
  62.6 30.5 %all_gather.13 = bf16[64,576]{1,0:T(8,128)(2,1)S(1)} all-gather(bf16[8,576]{1,0:T(8,128)(2,1)S(1)} %convert_element_type.126), channel_id=1, replica_groups=mesh['seq'=8,'tp'=4] {'seq'}, dimensions={0}, use_global_device_ids=true | all-gather | bytes 82944 | tf_op jit(solution)/shard_map/all_gather | solution.py:164
  93.2 0.2 convolution_convert_fusion.3
  93.4 0.8 copy.27
  94.2 3.2 %fusion.56 = (bf16[1,1,1024,576]{2,3,1,0:T(8,128)(2,1)}, bf16[1,1,1024,576]{2,3,1,0:T(8,128)(2,1)}) fusion(bf16[1,2,1024,576]{2,3,1,0:T(8,128)(2,1)} %param.17), kind=kLoop, calls=%fused_computation.104 | loop fusion | bytes 4718592 | tf_op jit(solution)/shard_map/slice | solution.py:49
  98.1 4.0 %copy.23 = bf16[512,1728]{0,1:T(8,128)(2,1)} copy(bf16[512,1728]{1,0:T(8,128)(2,1)} %slice.106) | data formatting | bytes 3538944 | tf_op jit(solution)/shard_map/slice | solution.py:150
  102.1 2.4 %fusion.57 = (bf16[512,1,576]{0,2,1:T(8,128)(2,1)}, bf16[512,1,576]{0,2,1:T(8,128)(2,1)S(1)}, bf16[512,1,576]{0,2,1:T(8,128)(2,1)S(1)}) fusion(bf16[512,3,576]{0,2,1:T(8,128)(2,1)} %bitcast.64), kind=kLoop, calls=%fused_computation.105 | loop fusion | bytes 3538944 | tf_op jit(solution)/shard_map/slice | solution.py:48
  104.5 1.2 convert.41
  105.6 0.3 multiply_cosine_fusion
  105.9 0.1 convert.40
  106.1 1.6 subtract_convert_fusion
  107.7 2.8 %fusion = (f32[9,512]{1,0:T(8,128)S(1)}, f32[9,512,1024]{2,1,0:T(8,128)S(1)}) fusion(pred[1024]{0:T(1024)(128)(4,1)S(1)} %iota_compare_fusion.3, bf16[1024,9,64]{0,2,1:T(8,128)(2,1)S(1)} %bitcast.67, bf16[512,9,32]{0,2,1:T(8,128)(2,1)S(1)} %get-tuple-element.17, bf16[512,9,32]{0,2,1:T(8,128)(2,1)S(1)} %get-tuple-element.18), kind=kOutput, calls=%fused_computation.3 | convolution fusion | flops 619310592 | bytes 20663296 | tf_op jit(solution)/shard_map/qhe,khe->hqk/dot_general | solution.py:52
  110.5 5.3 %fusion.3 = (f32[9,512]{1,0:T(8,128)S(1)}, f32[9,512,512]{1,2,0:T(8,128)}) fusion(pred[512,512]{0,1:T(8,128)(4,1)S(1)} %iota_compare_fusion, bf16[512,9,32]{0,2,1:T(8,128)(2,1)S(1)} %get-tuple-element.14, bf16[512,9,32]{0,2,1:T(8,128)(2,1)S(1)} %get-tuple-element.13, bf16[512,9,32]{0,2,1:T(8,128)(2,1)S(1)} %get-tuple-element.17, ...), kind=kOutput, calls=%fused_computation.9 | convolution fusion | flops 311422464 | bytes 10897408 | tf_op jit(solution)/shard_map/qhe,khe->hqk/dot_general | solution.py:56
  115.8 4.5 %fusion.1 = f32[9,512]{1,0:T(8,128)S(1)} fusion(f32[9,512,1024]{2,1,0:T(8,128)S(1)} %get-tuple-element.35, f32[9,512]{1,0:T(8,128)S(1)} %max.11, pred[1024]{0:T(1024)(128)(4,1)S(1)} %iota_compare_fusion.3), kind=kLoop, calls=%fused_computation.4 | loop fusion | flops 18869760 | bytes 18912256 | tf_op jit(solution)/shard_map/reduce_sum | solution.py:71
  120.4 5.6 %fusion.4 = f32[9,512]{1,0:T(8,128)S(1)} fusion(f32[9,512,512]{1,2,0:T(8,128)} %get-tuple-element.37, f32[9,512]{1,0:T(8,128)S(1)} %max.11, pred[512,512]{0,1:T(8,128)(4,1)S(1)} %iota_compare_fusion), kind=kLoop, calls=%fused_computation.10 | loop fusion | flops 9432576 | bytes 9736192 | tf_op jit(solution)/shard_map/reduce_sum | solution.py:71
  126.0 7.1 %fusion.16 = f32[512,9,64]{0,2,1:T(8,128)} fusion(bf16[1024,9,64]{0,2,1:T(8,128)(2,1)} %bitcast.71, f32[9,512,1024]{2,1,0:T(8,128)S(1)} %get-tuple-element.35, f32[9,512]{1,0:T(8,128)S(1)} %add.76, f32[9,512]{1,0:T(8,128)S(1)} %max.11, pred[1024]{0:T(1024)(128)(4,1)S(1)} %iota_compare_fusion.3), kind=kOutput, calls=%fused_computation.29 | convolution fusion | flops 627572736 | bytes 21271552 | tf_op jit(solution)/shard_map/hqk,khe->qhe/dot_general | solution.py:76
  133.1 6.0 %fusion.19 = bf16[512,9,64]{0,2,1:T(8,128)(2,1)S(1)} fusion(f32[512,9,64]{0,2,1:T(8,128)} %fusion.16, bf16[512,9,64]{0,2,1:T(8,128)(2,1)S(1)} %bitcast.72, f32[9,512,512]{1,2,0:T(8,128)} %get-tuple-element.37, f32[9,512]{1,0:T(8,128)S(1)} %add.76, f32[9,512]{1,0:T(8,128)S(1)} %max.11, pred[512,512]{0,1:T(8,128)(4,1)S(1)} %iota_compare_fusion), kind=kOutput, calls=%fused_computation.32 | convolution fusion | flops 314376192 | bytes 12095488 | tf_op jit(solution)/shard_map/hqk,khe->qhe/dot_general | solution.py:79
  139.1 3.5 %convolution_convert_fusion = bf16[520,2304]{1,0:T(8,128)(2,1)} fusion(bf16[576,2304]{1,0:T(8,128)(2,1)S(1)} %copy-done, bf16[8,576]{0,1:T(8,128)(2,1)S(1)} %copy-done.4, bf16[512,576]{0,1:T(8,128)(2,1)S(1)} %bitcast.74), kind=kOutput, calls=%fused_computation.24 | convolution fusion | flops 1382584320 | bytes 5649408 | tf_op jit(solution)/shard_map/dot_general | solution.py:169
  142.6 66.1 %all-gather.3.cloned.1.call-done = bf16[2080,2304]{1,0:T(8,128)(2,1)} async-done(((bf16[520,2304]{1,0:T(8,128)(2,1)}), bf16[2080,2304]{1,0:T(8,128)(2,1)}) %all-gather.3.cloned.1.call-update) | async-done | bytes 9584656 | tf_op jit(solution)/shard_map/all_gather | solution.py:170
  208.7 7.3 %reduce_sum.61 = bf16[520,2304]{1,0:T(8,128)(2,1)} reduce(bf16[4,520,2304]{2,1,0:T(8,128)(2,1)} %bitcast.62, bf16[]{:T(256)} %constant.34.clone.1), dimensions={0}, to_apply=%region_7.8 | reduce | flops 3594240 | bytes 11980802 | tf_op jit(solution)/shard_map/reduce_sum | solution.py:170
  216.1 3.4 %fusion.5 = (f32[520]{0:T(1024)S(1)}, bf16[520,2304]{1,0:T(8,128)(2,1)S(1)}) fusion(bf16[520,2304]{1,0:T(8,128)(2,1)} %reduce_sum.61, bf16[8,2304]{1,0:T(8,128)(2,1)S(1)} %copy-done.3, bf16[512,2304]{1,0:T(8,128)(2,1)} %param.11), kind=kLoop, calls=%fused_computation.16 | loop fusion | flops 11980280 | bytes 7190560 | tf_op jit(solution)/shard_map/reduce_sum | solution.py:15
  219.5 1.6 slice.122
  221.0 0.6 slice.123
  221.7 0.6 fusion.7
  222.3 1.6 slice.124
  223.8 0.6 slice.125
  (38 shorter events, 0.5 us)
Async XLA Ops:
  7.2 131.9 %copy-start = (bf16[576,2304]{1,0:T(8,128)(2,1)S(1)}, bf16[576,2304]{1,0:T(8,128)(2,1)}, u32[]{:S(2)}) copy-start(bf16[576,2304]{1,0:T(8,128)(2,1)} %param.15) | copy-start | bytes 7962628
  7.2 201.5 %all-gather.3.cloned.1.call-start = ((), (), s32[]{:S(2)}) async-start(), calls=%async_computation | async-start | bytes 11980800 | tf_op jit(solution)/shard_map/all_gather | solution.py:170
  8.8 12.5 %slice-start = ((s8[4718592]{0:T(1024)(128)(4,1)}), s8[4194304]{0:T(1024)(128)(4,1)S(1)}, s32[]{:S(2)}) async-start(s8[4718592]{0:T(1024)(128)(4,1)} %bitcast.65), calls=%async_computation.1 | async-start | bytes 8388608
  11.2 10.1 %slice-start.1 = ((s8[4718592]{0:T(1024)(128)(4,1)}), s8[524288]{0:T(1024)(128)(4,1)S(1)}, s32[]{:S(2)}) async-start(s8[4718592]{0:T(1024)(128)(4,1)} %bitcast.65), calls=%async_computation.2 | async-start | bytes 1048576
  21.3 35.1 %copy-start.6 = (s32[64]{0:T(128)S(1)}, s32[64]{0:T(128)}, u32[]{:S(2)}) copy-start(s32[64]{0:T(128)} %param.21) | copy-start | bytes 772
  105.6 2.1 copy-start.1
  126.0 7.1 %copy-start.2 = (bf16[512,1,576]{0,2,1:T(8,128)(2,1)S(1)}, bf16[512,1,576]{0,2,1:T(8,128)(2,1)}, u32[]{:S(2)}) copy-start(bf16[512,1,576]{0,2,1:T(8,128)(2,1)} %get-tuple-element.10) | copy-start | bytes 1769476
  133.1 6.0 %copy-start.4 = (bf16[8,576]{0,1:T(8,128)(2,1)S(1)}, bf16[8,576]{0,1:T(8,128)(2,1)}, u32[]{:S(2)}) copy-start(bf16[8,576]{0,1:T(8,128)(2,1)} %copy.27) | copy-start | bytes 27652
  208.7 7.3 %copy-start.3 = (bf16[8,2304]{1,0:T(8,128)(2,1)S(1)}, bf16[8,2304]{1,0:T(8,128)(2,1)}, u32[]{:S(2)}) copy-start(bf16[8,2304]{1,0:T(8,128)(2,1)} %param.12) | copy-start | bytes 110596
  216.1 5.6 %copy-start.5 = (f32[2304]{0:T(1024)S(1)}, f32[2304]{0:T(1024)}, u32[]{:S(2)}) copy-start(f32[2304]{0:T(1024)} %param.16) | copy-start | bytes 27652
Sparse Core Ops, SparseCore 0:
  142.7 65.9 all-gather.2
